TPU v7x, 256 devices: a whole 4x4x8 slice. The times are simulated.
256 devices in a mesh: clus: 32 (over y, z), tgt: 8 (over x, core).
Axes of the slice: x: 4, y: 4, z: 8, core: 2. Of those that a mesh axis runs over, the one named last changes fastest.
Arguments:
- weights_init: float32 [262144, 1024], P('clus', 'tgt'), may hold values from -6 to 6
- margins: float32 [4096, 1024], P('clus', 'tgt')
- block_bits: int32 [9216, 128, 8], P('clus'), may hold values from 0 to 65535
- block_run_index: int32 [9216], P('clus'), may hold values from 0 to 31, as said below
- block_col: int32 [9216], P('clus'), may hold values from 0 to 63
- block_tally: int32 [32], P('clus'), may hold values from 144 to 288, as said below
- step_size: float32 [1], replicated, may hold values from 0.3 to 0.6
- penalty: float32 [1], replicated, may hold values from 0.3 to 0.8
Outputs:
- weights: float32 [262144, 1024], P('clus', 'tgt')
- run_loss: float32 [4096], P('clus')
Inputs may be any that keep to these rules, and one draw needn't show every extreme that they name: `block_run_index`: A device's slots name distinct pairs of run block and cluster block. `block_tally`: some device's list is full in every draw.
All inputs are finite; a program needn't handle non-finite values.
Results may differ from a plain program's by a relative error of at most 0.0025.
Values may be sent and summed in bfloat16 or wider, within the bound.
No kernel may reach another device: no remote copies, remote signals or barrier semaphores. Data moves between devices by JAX's collectives and lax.ppermute only.
A program may use at most 128 MiB of HBM per device.

v0:
```python
import math
import jax
import jax.numpy as jnp
from jax import lax
from jax.sharding import PartitionSpec as P

BLOCK_ENTRIES = 128
TARGETS = 1024
ITERS = 2


def pick_blocks(index, count, table):
    selector = (index[:, None] == jnp.arange(count, dtype=jnp.int32)[None, :]).astype(table.dtype)
    flat = table.reshape(count, -1)
    picked = jnp.dot(selector, flat, preferred_element_type=jnp.float32).astype(table.dtype)
    return picked.reshape((index.shape[0],) + table.shape[1:])


def add_blocks(total, index, values):
    count = total.shape[0]
    selector = (jnp.arange(count, dtype=jnp.int32)[:, None] == index[None, :]).astype(jnp.float32)
    flat = values.reshape(index.shape[0], -1)
    summed = jnp.dot(
        selector, flat, preferred_element_type=jnp.float32, precision=lax.Precision.HIGHEST
    )
    return total + summed.reshape(total.shape)


def per_device(
    weights_init, margins, block_bits, block_run_index, block_col, block_tally, step_size, penalty
):
    slot_total = block_run_index.shape[0]
    nblocks = weights_init.shape[0] // BLOCK_ENTRIES
    tcols = weights_init.shape[1]
    ndev = lax.axis_size("clus")
    group_index = math.gcd(slot_total, 36)
    rotation_turns = slot_total // group_index
    live_slots = (jnp.arange(slot_total, dtype=jnp.int32) < block_tally[0]).astype(jnp.bfloat16)
    shifts = jnp.arange(16, dtype=jnp.int32)
    packed_flags = jnp.right_shift(block_bits[..., None], shifts) & 1
    sign_values = (2 * packed_flags - 1).astype(jnp.bfloat16).reshape(
        slot_total, BLOCK_ENTRIES, BLOCK_ENTRIES
    ) * live_slots[:, None, None]
    sign_groups = sign_values.reshape(rotation_turns, group_index, BLOCK_ENTRIES, BLOCK_ENTRIES)
    place_groups = block_run_index.reshape(rotation_turns, group_index)
    col_groups = block_col.reshape(rotation_turns, group_index)
    eta = step_size[0]
    thresh = eta * penalty[0]
    current = weights_init
    err = jnp.zeros((BLOCK_ENTRIES, tcols), jnp.float32)
    for step in range(ITERS):
        current_b = current.astype(jnp.bfloat16).reshape(nblocks, BLOCK_ENTRIES, tcols)

        def forward(total, portion):
            scan_inputs, pos, cols = portion
            selected_block = pick_blocks(cols, nblocks, current_b)
            product_rows = jnp.einsum(
                "vjs,vsh->vjh", scan_inputs, selected_block, preferred_element_type=jnp.float32
            )
            return (add_blocks(total, pos, product_rows), None)

        total, unused = lax.scan(
            forward,
            jnp.zeros((ndev, BLOCK_ENTRIES, tcols), jnp.float32),
            (sign_groups, place_groups, col_groups),
        )
        owned = lax.psum_scatter(
            total.reshape(ndev * BLOCK_ENTRIES, tcols).astype(jnp.bfloat16),
            "clus",
            scatter_dimension=0,
            tiled=True,
        ).astype(jnp.float32)
        err = owned / 128.0 - margins
        err_b = err.astype(jnp.bfloat16)
        residual_table = lax.all_gather(err_b, "clus", axis=0, tiled=True).reshape(
            ndev, BLOCK_ENTRIES, tcols
        )

        def backward(total, portion):
            scan_inputs, pos, cols = portion
            design_rows = pick_blocks(pos, ndev, residual_table)
            part = jnp.einsum(
                "oeq,oei->oqi", scan_inputs, design_rows, preferred_element_type=jnp.float32
            )
            return (add_blocks(total, cols, part), None)

        grads, unused = lax.scan(
            backward,
            jnp.zeros((nblocks, BLOCK_ENTRIES, tcols), jnp.float32),
            (sign_groups, place_groups, col_groups),
        )
        grad = grads.reshape(nblocks * BLOCK_ENTRIES, tcols) / 128.0
        moved = current - eta * grad
        current = jnp.sign(moved) * jnp.maximum(jnp.abs(moved) - thresh, 0.0)
    squares = jnp.sum(err * err, axis=1)
    run_loss = lax.psum(squares, "tgt") / TARGETS
    return (current, run_loss)


def solution(mesh):
    return jax.shard_map(
        per_device,
        mesh=mesh,
        in_specs=(
            P("clus", "tgt"),
            P("clus", "tgt"),
            P("clus", None, None),
            P("clus"),
            P("clus"),
            P("clus"),
            P(),
            P(),
        ),
        out_specs=(P("clus", "tgt"), P("clus")),
        check_vma=False,
    )
```

profile of v0, /device:TPU:2, one launch (start us, length us, event | category | flops | bytes accessed | tf_op | source)
XLA Modules:
  0.0 1006.4 jit_solution(12187850462215080191)
XLA Ops:
  8.0 9.2 shift_right_arithmetic.21
  17.2 14.9 %fusion.60 = bf16[8,36,128,128]{2,3,1,0:T(8,128)(2,1)} fusion(s32[8,36,128,128]{2,3,1,0:T(8,128)} %bitcast.215, s32[128]{0:T(128)S(1)} %shift_right_arithmetic.24, bf16[8,36]{1,0:T(8,128)(2,1)S(1)} %fusion.63), kind=kLoop, calls=%fused_computation.77 | loop fusion | flops 42467328 | bytes 28312640 | tf_op jit(solution)/shard_map/mul | solution.py:41
  32.1 12.7 %copy.20 = bf16[8,36,128,128]{3,2,1,0:T(8,128)(2,1)} copy(bf16[8,36,128,128]{2,3,1,0:T(8,128)(2,1)} %fusion.60) | data formatting | bytes 18874368
  45.0 2.4 convert_element_type.64
  47.4 2.7 reshape_reshape.16
  50.0 80.1 %while.48 = (s32[]{:T(128)}, f32[32,128,128]{2,0,1:T(8,128)}, s32[8,36]{1,0:T(8,128)S(1)}, bf16[8,36,128,128]{3,2,1,0:T(8,128)(2,1)}, s32[8,36]{1,0:T(8,128)S(1)...) while((s32[]{:T(128)}, f32[32,128,128]{2,0,1:T(8,128)}, ...), condition=%wide.wide.region_1.2_spmd.clone, body=%wide.wide.region_0.1_spmd.clone.sunk | while | flops 454626688 | bytes 21890508 | solution.py:62
  50.0 2.1 convolution_convert_fusion.12
  54.5 4.2 select_add_fusion.12
  58.7 2.1 convolution_convert_fusion.12
  63.1 5.7 select_add_fusion.12
  68.9 2.1 convolution_convert_fusion.12
  73.3 5.7 select_add_fusion.12
  79.1 2.1 convolution_convert_fusion.12
  83.6 5.7 select_add_fusion.12
  93.8 5.7 select_add_fusion.12
  99.5 2.1 convolution_convert_fusion.12
  104.0 5.7 select_add_fusion.12
  109.7 2.1 convolution_convert_fusion.12
  114.2 5.7 select_add_fusion.12
  120.0 2.1 convolution_convert_fusion.12
  124.4 5.7 select_add_fusion.12
  133.5 220.0 %reduce-scatter.3.cloned.1.call-done = bf16[128,128]{1,0:T(8,128)(2,1)} async-done(((bf16[4096,128]{1,0:T(8,128)(2,1)}), bf16[128,128]{1,0:T(8,128)(2,1)}) %reduce-scatter.3.cloned.1.call-update) | async-done | bytes 32784 | tf_op jit(solution)/shard_map/reduce_scatter | solution.py:67
  356.4 74.3 %all-gather.3.cloned.1.call-done = bf16[4096,128]{1,0:T(8,128)(2,1)} async-done(((bf16[128,128]{1,0:T(8,128)(2,1)}), bf16[4096,128]{1,0:T(8,128)(2,1)}) %all-gather.3.cloned.1.call-update) | async-done | bytes 1048592 | tf_op jit(solution)/shard_map/all_gather | solution.py:75
  432.3 83.9 %while.49 = (s32[]{:T(128)}, f32[64,128,128]{2,0,1:T(8,128)}, s32[8,36]{1,0:T(8,128)S(1)}, bf16[8,36,128,128]{2,3,1,0:T(8,128)(2,1)}, s32[8,36]{1,0:T(8,128)S(1)...) while((s32[]{:T(128)}, f32[64,128,128]{2,0,1:T(8,128)}, ...), condition=%wide.wide.region_4.5_spmd.clone, body=%wide.wide.region_3.4_spmd.clone.sunk | while | flops 644418944 | bytes 25036236 | solution.py:87
  435.2 5.7 select_add_fusion.13
  443.8 7.9 select_add_fusion.13
  454.5 7.9 select_add_fusion.13
  465.3 7.9 select_add_fusion.13
  476.1 7.9 select_add_fusion.13
  486.8 7.9 select_add_fusion.13
  497.6 7.9 select_add_fusion.13
  508.3 7.9 select_add_fusion.13
  516.2 2.6 broadcast_multiply_fusion.1
  518.9 2.4 copy.22
  525.2 2.7 reshape_reshape.20
  527.9 80.0 %while.50 = (s32[]{:T(128)}, f32[32,128,128]{2,0,1:T(8,128)}, s32[8,36]{1,0:T(8,128)S(1)}, bf16[8,36,128,128]{3,2,1,0:T(8,128)(2,1)}, s32[8,36]{1,0:T(8,128)S(1)...) while((s32[]{:T(128)}, f32[32,128,128]{2,0,1:T(8,128)}, ...), condition=%wide.wide.region_6.7_spmd.clone, body=%wide.wide.region_5.6_spmd.clone.sunk | while | flops 454626688 | bytes 21890508 | solution.py:62
  527.9 2.1 convolution_convert_fusion.14
  532.4 4.1 select_add_fusion.14
  536.5 2.1 convolution_convert_fusion.14
  541.0 5.7 select_add_fusion.14
  546.7 2.1 convolution_convert_fusion.14
  551.2 5.7 select_add_fusion.14
  556.9 2.1 convolution_convert_fusion.14
  561.4 5.7 select_add_fusion.14
  567.1 2.1 convolution_convert_fusion.14
  571.6 5.7 select_add_fusion.14
  581.8 5.7 select_add_fusion.14
  592.0 5.7 select_add_fusion.14
  602.2 5.7 select_add_fusion.14
  611.2 214.7 %reduce-scatter.5.cloned.1.call-done = bf16[128,128]{1,0:T(8,128)(2,1)} async-done(((bf16[4096,128]{1,0:T(8,128)(2,1)}), bf16[128,128]{1,0:T(8,128)(2,1)}) %reduce-scatter.5.cloned.1.call-update) | async-done | bytes 32784 | tf_op jit(solution)/shard_map/reduce_scatter | solution.py:67
  827.3 10.2 %psum.7 = f32[128]{0:T(128)S(1)} all-reduce(f32[128]{0:T(128)S(1)} %get-tuple-element.298), channel_id=1, replica_groups=mesh['clus'=32,'tgt'=8] {'tgt'}, use_global_device_ids=true, to_apply=%region_11.12 | all-reduce | flops 128 | bytes 1024 | tf_op jit(solution)/shard_map/psum | solution.py:96
  838.0 65.1 %all-gather.5.cloned.1.call-done = bf16[4096,128]{1,0:T(8,128)(2,1)} async-done(((bf16[128,128]{1,0:T(8,128)(2,1)}), bf16[4096,128]{1,0:T(8,128)(2,1)}) %all-gather.5.cloned.1.call-update) | async-done | bytes 1048592 | tf_op jit(solution)/shard_map/all_gather | solution.py:75
  904.6 83.9 %while.51 = (s32[]{:T(128)}, f32[64,128,128]{2,0,1:T(8,128)}, s32[8,36]{1,0:T(8,128)S(1)}, bf16[8,36,128,128]{2,3,1,0:T(8,128)(2,1)}, s32[8,36]{1,0:T(8,128)S(1)...) while((s32[]{:T(128)}, f32[64,128,128]{2,0,1:T(8,128)}, ...), condition=%wide.wide.region_9.10_spmd.clone, body=%wide.wide.region_8.9_spmd.clone.sunk | while | flops 644418944 | bytes 25036236 | solution.py:87
  907.5 5.7 select_add_fusion.15
  916.1 7.9 select_add_fusion.15
  926.8 7.9 select_add_fusion.15
  937.6 7.9 select_add_fusion.15
  948.4 7.9 select_add_fusion.15
  959.1 7.9 select_add_fusion.15
  969.9 7.9 select_add_fusion.15
  980.6 7.9 select_add_fusion.15
  988.5 2.6 broadcast_multiply_fusion
  991.2 2.4 copy.25
  994.6 5.3 maximum_multiply_fusion
  (193 shorter events, 109.0 us)
Async XLA Ops:
  7.2 346.3 %reduce-scatter.3.cloned.1.call-start = ((), (), s32[]{:S(2)}) async-start(), calls=%async_computation.2 | async-start | bytes 1081344 | tf_op jit(solution)/shard_map/reduce_scatter | solution.py:67
  32.1 12.7 %copy-start.7 = (s32[288]{0:T(512)S(1)}, s32[288]{0:T(512)}, u32[]{:S(2)}) copy-start(s32[288]{0:T(512)} %param.20) | copy-start | bytes 3460
  32.1 12.8 %copy-start.8 = (s32[288]{0:T(512)S(1)}, s32[288]{0:T(512)}, u32[]{:S(2)}) copy-start(s32[288]{0:T(512)} %param.19) | copy-start | bytes 3460
  47.4 2.7 copy-start.4
  130.2 223.3 %copy-start.6 = (f32[128,128]{1,0:T(8,128)S(1)}, f32[128,128]{1,0:T(8,128)}, u32[]{:S(2)}) copy-start(f32[128,128]{1,0:T(8,128)} %param.17) | copy-start | bytes 196612
  133.4 297.4 %all-gather.3.cloned.1.call-start = ((), (), s32[]{:S(2)}) async-start(), calls=%async_computation.3 | async-start | bytes 1081344 | tf_op jit(solution)/shard_map/all_gather | solution.py:75
  354.9 471.0 %reduce-scatter.5.cloned.1.call-start = ((), (), s32[]{:S(2)}) async-start(), calls=%async_computation.4 | async-start | bytes 1081344 | tf_op jit(solution)/shard_map/reduce_scatter | solution.py:67
  518.9 4.6 copy-start
  521.3 2.1 copy-start.2
  525.2 2.7 copy-start.5
  611.1 292.0 %all-gather.5.cloned.1.call-start = ((), (), s32[]{:S(2)}) async-start(), calls=%async_computation.5 | async-start | bytes 1081344 | tf_op jit(solution)/shard_map/all_gather | solution.py:75
  991.2 2.5 copy-start.1
  991.2 3.5 copy-start.3
Sparse Core Ops, SparseCore 0:
  133.5 219.8 reduce-scatter.2
  356.1 74.6 all-gather.2
  611.2 214.5 reduce-scatter.4
  828.3 74.7 all-gather.4
where the time goes:
time: 1010 us
  waiting for transfers between devices  574 us (57%)
  matrix products  309 us (31%)
  local copies, waits for them, and re-layouts  59.1 us (6%)
  other arithmetic  36.5 us (4%)
  between operations  15.9 us (2%)
  blocking collectives  10.2 us (1%)
    reduce_scatter x2, waiting for transfers between devices, per_device(): lax.psum_scatter(total.reshape(ndev * BLOCK_ENTRIES, tcols).astype(jnp.bf...  435 us
    dot_general x32, matrix products, add_blocks(): jnp.dot(selector, flat, preferred_element_type=jnp.float32, precision=lax...  211 us
    all_gather x2, waiting for transfers between devices, per_device(): lax.all_gather(err_b, 'clus', axis=0, tiled=True)  139 us
    dot_general x32, matrix products, pick_blocks(): jnp.dot(selector, flat, preferred_element_type=jnp.float32)  43 us
    dot_general x16, matrix products, forward(): jnp.einsum('vjs,vsh->vjh', scan_inputs, selected_block, preferred_element...  27.8 us
    dot_general x16, matrix products, backward(): jnp.einsum('oeq,oei->oqi', scan_inputs, design_rows, preferred_element_ty...  27.8 us
  transfers between devices with their start and end apart: 4, of which 4 were waited for; matrix products, arithmetic and copies ran while one was open for 0% of the time, Pallas kernels for 0%

commit v1 on v0

--- a/solution.py
+++ b/solution.py
@@ -72,9 +72,9 @@
         ).astype(jnp.float32)
         err = owned / 128.0 - margins
         err_b = err.astype(jnp.bfloat16)
-        residual_table = lax.all_gather(err_b, "clus", axis=0, tiled=True).reshape(
-            ndev, BLOCK_ENTRIES, tcols
-        )
+        residual_table = jnp.concatenate(
+            lax.all_to_all(jnp.stack([err_b] * lax.axis_size("clus")), "clus", 0, 0), axis=0
+        ).reshape(ndev, BLOCK_ENTRIES, tcols)
 
         def backward(total, portion):
             scan_inputs, pos, cols = portion

time: 1010 us -> 928 us (0.919)
  waiting for transfers between devices: 574 us -> 456 us
  starting transfers between devices: 0.34 us -> 25 us
    all_gather x2 -> x0, waiting for transfers between devices: 139 us -> none  [per_device(): lax.all_gather(err_b, 'clus', axis=0, tiled=True)]
    all_to_all x0 -> x2, waiting for transfers between devices: none -> 21.3 us  [per_device(): lax.all_to_all(jnp.stack([err_b] * lax.axis_size('clus')), 'clus', 0, 0)]
    all_to_all x0 -> x2, starting transfers between devices: none -> 13.6 us  [per_device(): lax.all_to_all(jnp.stack([err_b] * lax.axis_size('clus')), 'clus', 0, 0)]
    reduce_scatter x2, starting transfers between devices: 0.26 us -> 11.4 us  [per_device(): lax.psum_scatter(total.reshape(ndev * BLOCK_ENTRIES, tcols).astype(jnp.bf...]
where the time goes in v1:
time: 928 us; the launch traced here: 917 us
  waiting for transfers between devices  456 us (49%)
  matrix products  312 us (34%)
  local copies, waits for them, and re-layouts  63.4 us (7%)
  other arithmetic  31.7 us (3%)
  starting transfers between devices  25 us (3%)
  between operations  16.5 us (2%)
  blocking collectives  10.8 us (1%)
    reduce_scatter x2, waiting for transfers between devices, per_device(): lax.psum_scatter(total.reshape(ndev * BLOCK_ENTRIES, tcols).astype(jnp.bf...  435 us
    dot_general x32, matrix products, add_blocks(): jnp.dot(selector, flat, preferred_element_type=jnp.float32, precision=lax...  210 us
    dot_general x32, matrix products, pick_blocks(): jnp.dot(selector, flat, preferred_element_type=jnp.float32)  46.4 us
    dot_general x16, matrix products, forward(): jnp.einsum('vjs,vsh->vjh', scan_inputs, selected_block, preferred_element...  27.8 us
    dot_general x16, matrix products, backward(): jnp.einsum('oeq,oei->oqi', scan_inputs, design_rows, preferred_element_ty...  27.8 us
    all_to_all x2, waiting for transfers between devices, per_device(): lax.all_to_all(jnp.stack([err_b] * lax.axis_size('clus')), 'clus', 0, 0)  21.3 us
  transfers between devices with their start and end apart: 4, of which 4 were waited for; matrix products, arithmetic and copies ran while one was open for 0% of the time, Pallas kernels for 0%

profile of v1, /device:TPU:2, one launch (start us, length us, event | category | flops | bytes accessed | tf_op | source)
XLA Modules:
  0.0 916.8 jit_solution(12318478303862591857)
XLA Ops:
  8.0 9.2 %shift_right_arithmetic.21 = s32[288,128,8,16]{1,3,2,0:T(8,128)} broadcast(s32[288,128,8]{1,2,0:T(8,128)} %param.18), dimensions={0,1,2} | broadcast | bytes 20054016 | tf_op jit(solution)/shard_map/shift_right_arithmetic | solution.py:40
  17.2 14.9 %fusion.64 = bf16[8,36,128,128]{2,3,1,0:T(8,128)(2,1)} fusion(s32[8,36,128,128]{2,3,1,0:T(8,128)} %bitcast.211, s32[128]{0:T(128)S(1)} %shift_right_arithmetic.24, bf16[8,36]{1,0:T(8,128)(2,1)S(1)} %fusion.67), kind=kLoop, calls=%fused_computation.81 | loop fusion | flops 42467328 | bytes 28312640 | tf_op jit(solution)/shard_map/mul | solution.py:41
  32.1 12.7 %copy.18 = bf16[8,36,128,128]{3,2,1,0:T(8,128)(2,1)} copy(bf16[8,36,128,128]{2,3,1,0:T(8,128)(2,1)} %fusion.64) | data formatting | bytes 18874368
  44.9 2.4 convert_element_type.64
  47.3 2.7 reshape_reshape.8
  50.0 80.1 %while.48 = (s32[]{:T(128)}, f32[32,128,128]{2,0,1:T(8,128)}, s32[8,36]{1,0:T(8,128)S(1)}, bf16[8,36,128,128]{3,2,1,0:T(8,128)(2,1)}, s32[8,36]{1,0:T(8,128)S(1)...) while((s32[]{:T(128)}, f32[32,128,128]{2,0,1:T(8,128)}, ...), condition=%wide.wide.region_1.2_spmd.clone, body=%wide.wide.region_0.1_spmd.clone.sunk | while | flops 454626688 | bytes 21890508 | solution.py:62
  50.0 2.1 convolution_convert_fusion.12
  54.5 4.2 select_add_fusion.12
  58.7 2.1 convolution_convert_fusion.12
  63.1 5.7 select_add_fusion.12
  73.3 5.7 select_add_fusion.12
  79.1 2.1 convolution_convert_fusion.12
  83.6 5.7 select_add_fusion.12
  93.8 5.7 select_add_fusion.12
  99.5 2.1 convolution_convert_fusion.12
  104.0 5.7 select_add_fusion.12
  109.7 2.1 convolution_convert_fusion.12
  114.2 5.7 select_add_fusion.12
  120.0 2.1 convolution_convert_fusion.12
  124.4 5.7 select_add_fusion.12
  130.2 3.8 copy.65
  134.0 220.1 %reduce-scatter.3.cloned.1.call-done = bf16[128,128]{1,0:T(8,128)(2,1)} async-done(((bf16[4096,128]{1,0:T(8,128)(2,1)}), bf16[128,128]{1,0:T(8,128)(2,1)}) %reduce-scatter.3.cloned.1.call-update) | async-done | bytes 32784 | tf_op jit(solution)/shard_map/reduce_scatter | solution.py:67
  356.1 6.8 all-to-all-start
  362.9 11.4 %reduce-scatter.5.cloned.1.call-start = ((), (), s32[]{:S(2)}) async-start(), calls=%async_computation.5 | async-start | bytes 1081344 | tf_op jit(solution)/shard_map/reduce_scatter | solution.py:67
  375.6 9.8 %all-to-all-done = bf16[32,128,128]{2,1,0:T(8,128)(2,1)S(1)} async-done(((bf16[32,128,128]{2,1,0:T(8,128)(2,1)}), bf16[32,128,128]{2,1,0:T(8,128)(2,1)S(1)}, u32[]{:S(2)}, u32[]{:S(2)}) %all-to-all-start) | async-done | bytes 1048608 | tf_op jit(solution)/shard_map/all_to_all | solution.py:76
  385.4 85.6 %while.46 = (s32[]{:T(128)}, f32[64,128,128]{2,0,1:T(8,128)}, s32[8,36]{1,0:T(8,128)S(1)}, bf16[8,36,128,128]{2,3,1,0:T(8,128)(2,1)}, s32[8,36]{1,0:T(8,128)S(1)...) while((s32[]{:T(128)}, f32[64,128,128]{2,0,1:T(8,128)}, s32[8,36]{1,0:T(8,128)S(1)}, ...), condition=%wide.region_4.5_spmd.clone, body=%wide.region_3.4_spmd.clone.sunk | while | flops 644418944 | bytes 25036228 | solution.py:87
  388.5 5.7 select_add_fusion.10
  397.3 7.9 select_add_fusion.10
  408.2 7.9 select_add_fusion.10
  419.2 7.9 select_add_fusion.10
  430.2 7.9 select_add_fusion.10
  441.2 7.9 select_add_fusion.10
  452.1 7.9 select_add_fusion.10
  463.1 7.9 select_add_fusion.10
  471.0 2.6 broadcast_multiply_fusion.1
  473.6 2.4 copy.20
  479.9 2.7 reshape_reshape.10
  482.6 79.9 %while.49 = (s32[]{:T(128)}, f32[32,128,128]{2,0,1:T(8,128)}, s32[8,36]{1,0:T(8,128)S(1)}, bf16[8,36,128,128]{3,2,1,0:T(8,128)(2,1)}, s32[8,36]{1,0:T(8,128)S(1)...) while((s32[]{:T(128)}, f32[32,128,128]{2,0,1:T(8,128)}, ...), condition=%wide.wide.region_6.7_spmd.clone, body=%wide.wide.region_5.6_spmd.clone.sunk | while | flops 454626688 | bytes 21890508 | solution.py:62
  487.1 4.1 select_add_fusion.13
  491.2 2.1 convolution_convert_fusion.13
  495.7 5.7 select_add_fusion.13
  505.9 5.7 select_add_fusion.13
  516.0 5.7 select_add_fusion.13
  526.2 5.7 select_add_fusion.13
  536.4 5.7 select_add_fusion.13
  546.6 5.7 select_add_fusion.13
  556.8 5.7 select_add_fusion.13
  562.5 3.8 copy.64
  566.3 214.8 %reduce-scatter.5.cloned.1.call-done = bf16[128,128]{1,0:T(8,128)(2,1)} async-done(((bf16[4096,128]{1,0:T(8,128)(2,1)}), bf16[128,128]{1,0:T(8,128)(2,1)}) %reduce-scatter.5.cloned.1.call-update) | async-done | bytes 32784 | tf_op jit(solution)/shard_map/reduce_scatter | solution.py:67
  783.2 6.7 all-to-all-start.1
  789.9 10.8 %psum.7 = f32[128]{0:T(128)S(1)} all-reduce(f32[128]{0:T(128)S(1)} %get-tuple-element.298), channel_id=1, replica_groups=mesh['clus'=32,'tgt'=8] {'tgt'}, use_global_device_ids=true, to_apply=%region_11.12 | all-reduce | flops 128 | bytes 1024 | tf_op jit(solution)/shard_map/psum | solution.py:96
  801.2 11.5 %all-to-all-done.1 = bf16[32,128,128]{2,1,0:T(8,128)(2,1)S(1)} async-done(((bf16[32,128,128]{2,1,0:T(8,128)(2,1)}), bf16[32,128,128]{2,1,0:T(8,128)(2,1)S(1)}, u32[]{:S(2)}, u32[]{:S(2)}) %all-to-all-start.1) | async-done | bytes 1048608 | tf_op jit(solution)/shard_map/all_to_all | solution.py:76
  812.7 85.6 %while.47 = (s32[]{:T(128)}, f32[64,128,128]{2,0,1:T(8,128)}, s32[8,36]{1,0:T(8,128)S(1)}, bf16[8,36,128,128]{2,3,1,0:T(8,128)(2,1)}, s32[8,36]{1,0:T(8,128)S(1)...) while((s32[]{:T(128)}, f32[64,128,128]{2,0,1:T(8,128)}, s32[8,36]{1,0:T(8,128)S(1)}, ...), condition=%wide.region_9.10_spmd.clone, body=%wide.region_8.9_spmd.clone.sunk | while | flops 644418944 | bytes 25036228 | solution.py:87
  815.8 5.7 select_add_fusion.11
  824.6 7.9 select_add_fusion.11
  835.5 7.9 select_add_fusion.11
  846.5 7.9 select_add_fusion.11
  857.5 7.9 select_add_fusion.11
  868.5 7.9 select_add_fusion.11
  879.4 7.9 select_add_fusion.11
  890.4 7.9 select_add_fusion.11
  898.3 2.6 broadcast_multiply_fusion
  900.9 2.4 copy.23
  904.4 5.3 maximum_multiply_fusion
  (189 shorter events, 114.6 us)
Async XLA Ops:
  7.2 346.9 %reduce-scatter.3.cloned.1.call-start = ((), (), s32[]{:S(2)}) async-start(), calls=%async_computation.4 | async-start | bytes 1081344 | tf_op jit(solution)/shard_map/reduce_scatter | solution.py:67
  32.1 12.7 %copy-start.7 = (s32[288]{0:T(512)S(1)}, s32[288]{0:T(512)}, u32[]{:S(2)}) copy-start(s32[288]{0:T(512)} %param.20) | copy-start | bytes 3460
  32.1 12.8 %copy-start.8 = (s32[288]{0:T(512)S(1)}, s32[288]{0:T(512)}, u32[]{:S(2)}) copy-start(s32[288]{0:T(512)} %param.19) | copy-start | bytes 3460
  47.3 2.7 copy-start.4
  130.2 223.9 %copy-start.6 = (f32[128,128]{1,0:T(8,128)S(1)}, f32[128,128]{1,0:T(8,128)}, u32[]{:S(2)}) copy-start(f32[128,128]{1,0:T(8,128)} %param.17) | copy-start | bytes 196612
  356.1 29.3 %all-to-all-start = ((bf16[32,128,128]{2,1,0:T(8,128)(2,1)}), bf16[32,128,128]{2,1,0:T(8,128)(2,1)S(1)}, u32[]{:S(2)}, u32[]{:S(2)}) async-start(bf16[32,128,128]{2,1,0:T(8,128)(2,1)} %stack.4), calls=%async_computation.1 | async-start | bytes 2097152 | tf_op jit(solution)/shard_map/all_to_all | solution.py:76
  362.9 418.1 %reduce-scatter.5.cloned.1.call-start = ((), (), s32[]{:S(2)}) async-start(), calls=%async_computation.5 | async-start | bytes 1081344 | tf_op jit(solution)/shard_map/reduce_scatter | solution.py:67
  473.6 4.5 copy-start
  476.0 2.1 copy-start.2
  479.9 2.7 copy-start.5
  783.2 29.5 %all-to-all-start.1 = ((bf16[32,128,128]{2,1,0:T(8,128)(2,1)}), bf16[32,128,128]{2,1,0:T(8,128)(2,1)S(1)}, u32[]{:S(2)}, u32[]{:S(2)}) async-start(bf16[32,128,128]{2,1,0:T(8,128)(2,1)} %stack.5), calls=%async_computation.3 | async-start | bytes 2097152 | tf_op jit(solution)/shard_map/all_to_all | solution.py:76
  900.9 2.5 copy-start.1
  900.9 3.5 copy-start.3
Sparse Core Ops, SparseCore 0:
  134.1 219.9 reduce-scatter.2
  566.5 214.5 reduce-scatter.4
